TPU v7x, 128 devices: a whole 4x4x4 slice. The times are simulated.
128 devices in a mesh: rcv: 16 (over x_hi, y, core), src: 8 (over z, x_lo).
Axes of the slice: x: 4 (x_hi: 2, x_lo: 2; x = x_hi * 2 + x_lo), y: 4, z: 4, core: 2. Of those that a mesh axis runs over, the one named last changes fastest.
Arguments:
- kernel_codes: bfloat16 [2, 8192, 65536], P(None, 'rcv', 'src'), may hold values from -128 to 127
- kernel_exps: int32 [8192, 512], P('rcv', 'src'), may hold values from -17 to -14
- wavefield: bfloat16 [2, 65536, 128], P(None, 'src', 'rcv'), may hold values from -6 to 6
- observed: bfloat16 [2, 8192, 128], P(None, 'rcv'), may hold values from -6 to 6
- receiver_mask: int32 [8192], P('rcv'), may hold values 0 or 1
Outputs:
- residual: bfloat16 [2, 8192, 128], P(None, 'rcv', 'src')
- gradient: bfloat16 [2, 65536, 128], P(None, 'src', 'rcv')
All inputs are finite; a program needn't handle non-finite values. No bound on the sum of `receiver_mask` on one device may be relied on, other than what follows from the above.
Results may differ from a plain program's by a relative error of at most 0.0049.
Values may be sent and summed in bfloat16 or wider, within the bound.
No kernel may reach another device: no remote copies, remote signals or barrier semaphores. Data moves between devices by JAX's collectives and lax.ppermute only.
A program may use at most 128 MiB of HBM per device.

v0:
```python
import jax
import jax.numpy as jnp
from jax import lax
from jax.sharding import PartitionSpec as P

EXP_BLOCK = 128


def decode(codes, exps):
    rows = codes.shape[1]
    cols = codes.shape[2]
    scale = jnp.exp2(exps.astype(jnp.float32))[:, :, None]

    def widen(values):
        blocks = values.reshape(rows, cols // EXP_BLOCK, EXP_BLOCK).astype(jnp.float32) * scale
        return blocks.reshape(rows, cols).astype(jnp.bfloat16)

    return jnp.concatenate([widen(codes[0]), widen(codes[1])], axis=0)


def body(kernel_codes, kernel_exps, wavefield, observed, receiver_mask):
    rows = kernel_codes.shape[1]
    n_src = lax.axis_size("src")
    stacked = decode(kernel_codes, kernel_exps)
    piece = lax.all_gather(wavefield, "rcv", axis=2, tiled=True)
    span = piece.shape[2]
    joined = jnp.concatenate([piece[0], piece[1]], axis=1)
    prod = jnp.dot(stacked, joined, preferred_element_type=jnp.float32)
    pred_real = prod[:rows, :span] - prod[rows:, span:]
    pred_imag = prod[:rows, span:] + prod[rows:, :span]
    partial_pred = jnp.stack([pred_real, pred_imag])
    width = partial_pred.shape[2]
    share_cols = width // n_src
    live = receiver_mask.astype(jnp.float32)[None, :, None]
    predicted = lax.psum(partial_pred, "src")
    resid = (live * (predicted - observed.astype(jnp.float32))).astype(jnp.bfloat16)
    own_resid = lax.dynamic_slice_in_dim(resid, lax.axis_index("src") * share_cols, share_cols, 2)
    left = jnp.concatenate([resid[0], resid[1]], axis=0)
    right = jnp.concatenate([resid[1], -resid[0]], axis=0)
    grad_real = lax.dot_general(
        stacked, left, (((0,), (0,)), ((), ())), preferred_element_type=jnp.float32
    )
    grad_imag = lax.dot_general(
        stacked, right, (((0,), (0,)), ((), ())), preferred_element_type=jnp.float32
    )
    summed = lax.psum_scatter(
        jnp.stack([grad_real, grad_imag]), "rcv", scatter_dimension=2, tiled=True
    )
    gradient = summed.astype(jnp.bfloat16)
    return (own_resid, gradient)


def solution(mesh):
    in_specs = (
        P(None, "rcv", "src"),
        P("rcv", "src"),
        P(None, "src", "rcv"),
        P(None, "rcv", None),
        P("rcv"),
    )
    out_specs = (P(None, "rcv", "src"), P(None, "src", "rcv"))
    return jax.shard_map(body, mesh=mesh, in_specs=in_specs, out_specs=out_specs, check_vma=False)
```

profile of v0, /device:TPU:0, one launch (start us, length us, event | category | flops | bytes accessed | tf_op | source)
XLA Modules:
  0.0 313.3 jit_solution(1897431621627236321)
XLA Ops:
  7.2 0.0 all-gather.2.cloned.1.call-start
  7.2 0.7 all-gather.2.cloned.1.call-update
  7.9 0.0 all-reduce.4.cloned.1.call-start
  7.9 0.9 multiply_exponential_fusion
  8.9 0.1 copy.10
  9.0 4.6 %mul.30 = f32[512,64,128]{2,1,0:T(8,128)S(1)} broadcast(f32[512,64]{1,0:T(8,128)S(1)} %copy.10), dimensions={0,1} | broadcast | bytes 16908288 | tf_op jit(solution)/shard_map/mul | solution.py:15
  13.6 18.3 %fusion = (bf16[512,8192]{1,0:T(8,128)(2,1)}, bf16[512,8192]{1,0:T(8,128)(2,1)}) fusion(f32[64,8,64,128]{3,2,1,0:T(8,128)S(1)} %bitcast.33, bf16[2,512,8192]{2,1,0:T(8,128)(2,1)} %param.5), kind=kLoop, calls=%fused_computation.2 | loop fusion | flops 25165824 | bytes 50331648 | tf_op jit(solution)/shard_map/convert_element_type | solution.py:16
  32.0 35.8 %all-gather.2.cloned.1.call-done = bf16[2,8192,128]{1,2,0:T(8,128)(2,1)} async-done(((bf16[2,8192,8]{1,2,0:T(8,128)(2,1)}), bf16[2,8192,128]{1,2,0:T(8,128)(2,1)}) %all-gather.2.cloned.1.call-update) | async-done | bytes 4194320 | tf_op jit(solution)/shard_map/all_gather | solution.py:25
  67.7 0.0 copy-start
  67.7 4.1 %slice_bitcast_fusion.1 = (bf16[8192,128]{0,1:T(8,128)(2,1)S(1)}, bf16[8192,128]{0,1:T(8,128)(2,1)}) fusion(bf16[2,8192,128]{1,2,0:T(8,128)(2,1)} %all-gather.2.cloned.1.call-done), kind=kLoop, calls=%fused_computation.13 | loop fusion | bytes 8388608 | tf_op jit(solution)/shard_map/squeeze | solution.py:27
  71.8 1.3 copy-done
  73.1 0.0 copy-start.2
  73.1 0.0 copy-start.3
  73.1 0.0 copy-start.1
  73.1 9.5 %fusion.2 = f32[1024,256]{1,0:T(8,128)} fusion(bf16[512,8192]{1,0:T(8,128)(2,1)} %get-tuple-element.7, bf16[512,8192]{1,0:T(8,128)(2,1)S(1)} %copy-done, bf16[8192,128]{0,1:T(8,128)(2,1)} %get-tuple-element.9, bf16[8192,128]{0,1:T(8,128)(2,1)S(1)} %get-tuple-element.8), kind=kOutput, calls=%fused_computation.8 | convolution fusion | flops 4336910336 | bytes 22020096 | tf_op jit(solution)/shard_map/dot_general | solution.py:28
  82.7 1.2 fusion.7
  83.9 0.8 pad_maximum_fusion.5
  84.7 0.0 all-reduce.4.cloned.1.call-update
  84.8 0.0 copy-done.2
  84.8 0.0 copy-done.3
  84.8 0.6 dynamic-slice
  86.1 73.1 %all-reduce.4.cloned.1.call-done = f32[2,512,128]{2,1,0:T(8,128)} async-done(((f32[2,512,128]{2,1,0:T(8,128)}), f32[2,512,128]{2,1,0:T(8,128)}) %all-reduce.4.cloned.1.call-update) | async-done | bytes 524304 | tf_op jit(solution)/shard_map/psum | solution.py:35
  159.2 0.0 copy-done.1
  159.2 0.0 slice-start
  159.2 0.0 slice-start.2
  159.2 1.3 multiply_convert_fusion
  160.6 0.0 slice-start.1
  160.6 0.0 slice-start.3
  160.6 10.2 %convolution_bitcast_fusion.1 = f32[1,8192,128]{2,1,0:T(8,128)} fusion(bf16[512,8192]{1,0:T(8,128)(2,1)} %get-tuple-element.7, bf16[512,8192]{1,0:T(8,128)(2,1)} %get-tuple-element.6, bf16[512,128]{1,0:T(8,128)(2,1)S(1)} %get-tuple-element.13, bf16[512,128]{1,0:T(8,128)(2,1)S(1)} %get-tuple-element.12), kind=kOutput, calls=%fused_computation.6 | convolution fusion | flops 2181562368 | bytes 21233664 | tf_op jit(solution)/shard_map/dot_general | solution.py:40
  170.8 0.0 slice-done
  170.8 0.0 slice-done.2
  170.9 0.0 slice-done.1
  170.9 0.9 slice-done.3
  171.7 6.3 %convolution_bitcast_fusion = f32[1,8192,128]{2,1,0:T(8,128)} fusion(bf16[512,8192]{1,0:T(8,128)(2,1)S(1)} %bitcast.37, bf16[512,8192]{1,0:T(8,128)(2,1)S(1)} %bitcast.35, bf16[512,128]{1,0:T(8,128)(2,1)S(1)} %fusion.17, bf16[512,128]{1,0:T(8,128)(2,1)S(1)} %get-tuple-element.13), kind=kOutput, calls=%fused_computation.5 | convolution fusion | flops 2181562368 | bytes 21233664 | tf_op jit(solution)/shard_map/dot_general | solution.py:43
  178.0 7.2 %pad_maximum_fusion.1 = f32[2,8192,128]{2,1,0:T(8,128)} fusion(f32[1,8192,128]{2,1,0:T(8,128)} %convolution_bitcast_fusion, f32[1,8192,128]{2,1,0:T(8,128)} %convolution_bitcast_fusion.1), kind=kLoop, calls=%fused_computation.7 | loop fusion | flops 2097152 | bytes 16777216 | tf_op jit(solution)/shard_map/stack | solution.py:47
  185.2 13.2 %copy.11 = f32[2,8192,128]{1,0,2:T(2,128)} copy(f32[2,8192,128]{2,1,0:T(8,128)} %pad_maximum_fusion.1) | data formatting | bytes 16777216 | tf_op jit(solution)/shard_map/stack | solution.py:47
  198.4 105.1 %all-reduce.5 = bf16[2,8192,128]{1,0,2:T(2,128)(2,1)} all-reduce(f32[2,8192,128]{1,0,2:T(2,128)} %copy.11), channel_id=2, replica_groups=mesh['rcv'=16,'src'=8] {'rcv'}, use_global_device_ids=true, to_apply=%region_1.0.clone | all-reduce | flops 2097152 | bytes 12582912
  303.6 1.1 dynamic-slice_convert_fusion
  304.7 0.9 copy.13
  305.6 0.1 constant_dynamic-slice_fusion
  305.7 0.7 copy.12
  (5 shorter events, 0.0 us)
Async XLA Ops:
  7.2 60.6 %all-gather.2.cloned.1.call-start = ((), (), s32[]{:S(2)}) async-start(), calls=%async_computation | async-start | bytes 4456448 | tf_op jit(solution)/shard_map/all_gather | solution.py:25
  7.9 151.3 %all-reduce.4.cloned.1.call-start = ((), (), s32[]{:S(2)}) async-start(), calls=%async_computation.1 | async-start | bytes 1048576 | tf_op jit(solution)/shard_map/psum | solution.py:35
  67.7 5.4 %copy-start = (bf16[512,8192]{1,0:T(8,128)(2,1)S(1)}, bf16[512,8192]{1,0:T(8,128)(2,1)}, u32[]{:S(2)}) copy-start(bf16[512,8192]{1,0:T(8,128)(2,1)} %get-tuple-element.6) | copy-start | bytes 25165828
  73.1 11.7 %copy-start.2 = (s32[512]{0:T(512)S(1)}, s32[512]{0:T(512)}, u32[]{:S(2)}) copy-start(s32[512]{0:T(512)} %param.9) | copy-start | bytes 6148
  73.1 11.7 %copy-start.3 = (u32[128]{0:T(128)S(1)}, u32[128]{0:T(128)}, u32[]{:S(2)}) copy-start(u32[128]{0:T(128)} %constant.15) | copy-start | bytes 1540
  73.1 86.1 %copy-start.1 = (bf16[2,512,128]{2,1,0:T(8,128)(2,1)S(1)}, bf16[2,512,128]{2,1,0:T(8,128)(2,1)}, u32[]{:S(2)}) copy-start(bf16[2,512,128]{2,1,0:T(8,128)(2,1)} %param.8) | copy-start | bytes 786436
  159.2 11.6 %slice-start = ((s8[8388608]{0:T(1024)(128)(4,1)}), s8[4194304]{0:T(1024)(128)(4,1)S(1)}, s32[]{:S(2)}) async-start(s8[8388608]{0:T(1024)(128)(4,1)} %bitcast.34), calls=%async_computation.2 | async-start | bytes 8388608
  159.2 11.6 %slice-start.2 = ((s8[8388608]{0:T(1024)(128)(4,1)}), s8[4194304]{0:T(1024)(128)(4,1)S(1)}, s32[]{:S(2)}) async-start(s8[8388608]{0:T(1024)(128)(4,1)} %bitcast.36), calls=%async_computation.4 | async-start | bytes 8388608
  160.6 10.3 %slice-start.1 = ((s8[8388608]{0:T(1024)(128)(4,1)}), s8[4194304]{0:T(1024)(128)(4,1)S(1)}, s32[]{:S(2)}) async-start(s8[8388608]{0:T(1024)(128)(4,1)} %bitcast.34), calls=%async_computation.3 | async-start | bytes 8388608
  160.6 11.1 %slice-start.3 = ((s8[8388608]{0:T(1024)(128)(4,1)}), s8[4194304]{0:T(1024)(128)(4,1)S(1)}, s32[]{:S(2)}) async-start(s8[8388608]{0:T(1024)(128)(4,1)} %bitcast.36), calls=%async_computation.5 | async-start | bytes 8388608
Sparse Core Ops, SparseCore 0:
  10.5 57.1 all-gather.1
  84.9 74.2 all-reduce.3
where the time goes:
time: 314 us; the launch traced here: 313 us
  waiting for transfers between devices  110 us (35%)
  blocking collectives  105 us (33%)
  other arithmetic  29.9 us (10%)
  local copies, waits for them, and re-layouts  27.7 us (9%)
  matrix products  26 us (8%)
  between operations  14.8 us (5%)
    unnamed x1, blocking collectives  105 us
    psum x1, waiting for transfers between devices, body(): predicted = lax.psum(partial_pred, 'src')  73.1 us
    all_gather x1, waiting for transfers between devices, body(): piece = lax.all_gather(wavefield, 'rcv', axis=2, tiled=True)  35.8 us
    convert_element_type x1, other arithmetic, widen(): return blocks.reshape(rows, cols).astype(jnp.bfloat16)  18.3 us
    another operation x1, local copies, waits for them, and re-layouts, body(): jnp.stack([grad_real, grad_imag])  13.2 us
    dot_general x1, matrix products, body(): lax.dot_general(stacked, left, (((0,), (0,)), ((), ())), preferred_elemen...  10.2 us
    dot_general x1, matrix products, body(): prod = jnp.dot(stacked, joined, preferred_element_type=jnp.float32)  9.54 us
    another operation x1, other arithmetic, body(): jnp.stack([grad_real, grad_imag])  7.24 us
  transfers between devices with their start and end apart: 2, of which 2 were waited for; matrix products, arithmetic and copies ran while one was open for 8% of the time, Pallas kernels for 0%

commit v1 on v0

--- a/solution.py
+++ b/solution.py
@@ -2,6 +2,7 @@
 import jax.numpy as jnp
 from jax import lax
 from jax.sharding import PartitionSpec as P
+from jax.lax import all_to_all, axis_size
 
 EXP_BLOCK = 128
 
@@ -22,7 +23,10 @@
     rows = kernel_codes.shape[1]
     n_src = lax.axis_size("src")
     stacked = decode(kernel_codes, kernel_exps)
-    piece = lax.all_gather(wavefield, "rcv", axis=2, tiled=True)
+    piece = jnp.concatenate(
+        all_to_all(jnp.stack([wavefield] * axis_size("rcv")), "rcv", split_axis=0, concat_axis=0),
+        axis=2,
+    )
     span = piece.shape[2]
     joined = jnp.concatenate([piece[0], piece[1]], axis=1)
     prod = jnp.dot(stacked, joined, preferred_element_type=jnp.float32)

time: 314 us -> 330 us (1.051)
  starting transfers between devices: 0.08 us -> 7.24 us
  waiting for transfers between devices: 110 us -> 116 us
    all_gather x1 -> x0, waiting for transfers between devices: 35.8 us -> none  [body(): piece = lax.all_gather(wavefield, 'rcv', axis=2, tiled=True)]
    all_to_all x0 -> x1, waiting for transfers between devices: none -> 32.7 us  [body(): all_to_all(jnp.stack([wavefield] * axis_size('rcv')), 'rcv', split_axis=0...]
    psum x1, waiting for transfers between devices: 73.1 us -> 83.1 us  [body(): predicted = lax.psum(partial_pred, 'src')]
    all_to_all x0 -> x1, starting transfers between devices: none -> 7.2 us  [body(): all_to_all(jnp.stack([wavefield] * axis_size('rcv')), 'rcv', split_axis=0...]
    another operation x0 -> x1, local copies, waits for them, and re-layouts: none -> 3.44 us  [body(): jnp.stack([wavefield] * axis_size('rcv'))]
  transfers between devices with their start and end apart: 2 -> 2, of which waited for: 2 -> 2; matrix products, arithmetic and copies ran while one was open for 8% -> 7% of each run, Pallas kernels for 0% -> 0%
where the time goes in v1:
time: 330 us; the launch traced here: 329 us
  waiting for transfers between devices  116 us (35%)
  blocking collectives  105 us (32%)
  local copies, waits for them, and re-layouts  30.7 us (9%)
  other arithmetic  29 us (9%)
  matrix products  26.3 us (8%)
  between operations  14.9 us (5%)
  starting transfers between devices  7.24 us (2%)
    unnamed x1, blocking collectives  105 us
    psum x1, waiting for transfers between devices, body(): predicted = lax.psum(partial_pred, 'src')  83.1 us
    all_to_all x1, waiting for transfers between devices, body(): all_to_all(jnp.stack([wavefield] * axis_size('rcv')), 'rcv', split_axis=0...  32.7 us
    convert_element_type x1, other arithmetic, widen(): return blocks.reshape(rows, cols).astype(jnp.bfloat16)  18.3 us
    another operation x1, local copies, waits for them, and re-layouts, body(): jnp.stack([grad_real, grad_imag])  13.3 us
    dot_general x1, matrix products, body(): lax.dot_general(stacked, left, (((0,), (0,)), ((), ())), preferred_elemen...  10.5 us
    dot_general x1, matrix products, body(): prod = jnp.dot(stacked, joined, preferred_element_type=jnp.float32)  9.54 us
    another operation x1, other arithmetic, body(): jnp.stack([grad_real, grad_imag])  7.24 us
  transfers between devices with their start and end apart: 2, of which 2 were waited for; matrix products, arithmetic and copies ran while one was open for 7% of the time, Pallas kernels for 0%

profile of v1, /device:TPU:0, one launch (start us, length us, event | category | flops | bytes accessed | tf_op | source)
XLA Modules:
  0.0 329.0 jit_solution(3009141171338126210)
XLA Ops:
  7.2 0.0 copy-start.1
  7.2 3.4 %stack.14 = bf16[16,2,8192,8]{2,3,1,0:T(8,128)(2,1)} broadcast(bf16[2,8192,8]{1,2,0:T(8,128)(2,1)} %param.7), dimensions={1,2,3} | broadcast | bytes 4456448 | tf_op jit(solution)/shard_map/stack | solution.py:27
  10.6 7.2 %all-to-all-start = ((bf16[16,2,8192,8]{2,3,1,0:T(8,128)(2,1)}), bf16[16,2,8192,8]{2,3,1,0:T(8,128)(2,1)}, u32[]{:S(2)}, u32[]{:S(2)}) async-start(bf16[16,2,8192,8]{2,3,1,0:T(8,128)(2,1)} %stack.14), calls=%async_computation | async-start | bytes 8388608 | tf_op jit(solution)/shard_map/all_to_all | solution.py:27
  17.8 0.0 all-reduce.4.cloned.1.call-start
  17.9 0.0 copy-done.1
  17.9 0.1 copy.14
  18.0 4.6 %mul.30 = f32[512,64,128]{2,1,0:T(8,128)S(1)} broadcast(f32[512,64]{1,0:T(8,128)S(1)} %copy.14), dimensions={0,1} | broadcast | bytes 16908288 | tf_op jit(solution)/shard_map/mul | solution.py:16
  22.7 18.3 %fusion = (bf16[512,8192]{1,0:T(8,128)(2,1)}, bf16[512,8192]{1,0:T(8,128)(2,1)}) fusion(f32[64,8,64,128]{3,2,1,0:T(8,128)S(1)} %bitcast.36, bf16[2,512,8192]{2,1,0:T(8,128)(2,1)} %param.5), kind=kLoop, calls=%fused_computation.2 | loop fusion | flops 25165824 | bytes 50331648 | tf_op jit(solution)/shard_map/convert_element_type | solution.py:17
  41.0 32.7 %all-to-all-done = bf16[16,2,8192,8]{2,3,1,0:T(8,128)(2,1)} async-done(((bf16[16,2,8192,8]{2,3,1,0:T(8,128)(2,1)}), bf16[16,2,8192,8]{2,3,1,0:T(8,128)(2,1)}, u32[]{:S(2)}, u32[]{:S(2)}) %all-to-all-start) | async-done | bytes 4194336 | tf_op jit(solution)/shard_map/all_to_all | solution.py:27
  73.7 0.0 slice-start
  73.7 2.6 copy.23
  76.3 0.0 slice-start.1
  76.3 1.6 slice_bitcast_fusion.1
  78.0 0.0 slice-done
  78.0 1.5 slice-done.1
  79.5 0.0 copy-start.2
  79.5 0.0 copy-start.3
  79.5 0.0 copy-start
  79.5 9.5 %fusion.2 = f32[1024,256]{1,0:T(8,128)} fusion(bf16[512,8192]{1,0:T(8,128)(2,1)} %get-tuple-element.9, bf16[512,8192]{1,0:T(8,128)(2,1)S(1)} %bitcast.39, bf16[8192,128]{0,1:T(8,128)(2,1)} %get-tuple-element.11, bf16[8192,128]{0,1:T(8,128)(2,1)S(1)} %get-tuple-element.10), kind=kOutput, calls=%fused_computation.8 | convolution fusion | flops 4336910336 | bytes 22020096 | tf_op jit(solution)/shard_map/dot_general | solution.py:32
  89.0 1.2 fusion.7
  90.2 0.8 pad_maximum_fusion.5
  91.1 0.0 all-reduce.4.cloned.1.call-update
  91.1 0.0 copy-done.2
  91.1 0.0 copy-done.3
  91.2 0.6 dynamic-slice
  92.4 83.1 %all-reduce.4.cloned.1.call-done = f32[2,512,128]{2,1,0:T(8,128)} async-done(((f32[2,512,128]{2,1,0:T(8,128)}), f32[2,512,128]{2,1,0:T(8,128)}) %all-reduce.4.cloned.1.call-update) | async-done | bytes 524304 | tf_op jit(solution)/shard_map/psum | solution.py:39
  175.5 0.0 copy-done
  175.5 0.0 slice-start.2
  175.5 0.0 slice-start.4
  175.5 1.3 multiply_convert_fusion
  176.9 0.0 slice-start.3
  176.9 0.0 slice-start.5
  176.9 10.5 %convolution_bitcast_fusion.1 = f32[1,8192,128]{2,1,0:T(8,128)} fusion(bf16[512,8192]{1,0:T(8,128)(2,1)} %get-tuple-element.9, bf16[512,8192]{1,0:T(8,128)(2,1)} %get-tuple-element.8, bf16[512,128]{1,0:T(8,128)(2,1)S(1)} %get-tuple-element.15, bf16[512,128]{1,0:T(8,128)(2,1)S(1)} %get-tuple-element.14), kind=kOutput, calls=%fused_computation.6 | convolution fusion | flops 2181562368 | bytes 21233664 | tf_op jit(solution)/shard_map/dot_general | solution.py:44
  187.3 0.0 slice-done.2
  187.3 0.0 slice-done.4
  187.4 0.0 slice-done.3
  187.4 0.0 slice-done.5
  187.4 6.3 %convolution_bitcast_fusion = f32[1,8192,128]{2,1,0:T(8,128)} fusion(bf16[512,8192]{1,0:T(8,128)(2,1)S(1)} %bitcast.43, bf16[512,8192]{1,0:T(8,128)(2,1)S(1)} %bitcast.41, bf16[512,128]{1,0:T(8,128)(2,1)S(1)} %fusion.17, bf16[512,128]{1,0:T(8,128)(2,1)S(1)} %get-tuple-element.15), kind=kOutput, calls=%fused_computation.5 | convolution fusion | flops 2181562368 | bytes 21233664 | tf_op jit(solution)/shard_map/dot_general | solution.py:47
  193.7 7.2 %pad_maximum_fusion.1 = f32[2,8192,128]{2,1,0:T(8,128)} fusion(f32[1,8192,128]{2,1,0:T(8,128)} %convolution_bitcast_fusion, f32[1,8192,128]{2,1,0:T(8,128)} %convolution_bitcast_fusion.1), kind=kLoop, calls=%fused_computation.7 | loop fusion | flops 2097152 | bytes 16777216 | tf_op jit(solution)/shard_map/stack | solution.py:51
  200.9 13.3 %copy.16 = f32[2,8192,128]{1,0,2:T(2,128)} copy(f32[2,8192,128]{2,1,0:T(8,128)} %pad_maximum_fusion.1) | data formatting | bytes 16777216 | tf_op jit(solution)/shard_map/stack | solution.py:51
  214.2 105.1 %all-reduce.5 = bf16[2,8192,128]{1,0,2:T(2,128)(2,1)} all-reduce(f32[2,8192,128]{1,0,2:T(2,128)} %copy.16), channel_id=2, replica_groups=mesh['rcv'=16,'src'=8] {'rcv'}, use_global_device_ids=true, to_apply=%region_1.0.clone | all-reduce | flops 2097152 | bytes 12582912
  319.3 1.1 dynamic-slice_convert_fusion
  320.4 0.9 copy.18
  321.3 0.1 constant_dynamic-slice_fusion
  321.4 0.7 copy.17
  (7 shorter events, 0.1 us)
Async XLA Ops:
  7.2 10.7 %copy-start.1 = (s32[512,64]{0,1:T(8,128)S(1)}, s32[512,64]{0,1:T(8,128)}, u32[]{:S(2)}) copy-start(s32[512,64]{0,1:T(8,128)} %param.6) | copy-start | bytes 393220
  10.6 63.1 %all-to-all-start = ((bf16[16,2,8192,8]{2,3,1,0:T(8,128)(2,1)}), bf16[16,2,8192,8]{2,3,1,0:T(8,128)(2,1)}, u32[]{:S(2)}, u32[]{:S(2)}) async-start(bf16[16,2,8192,8]{2,3,1,0:T(8,128)(2,1)} %stack.14), calls=%async_computation | async-start | bytes 8388608 | tf_op jit(solution)/shard_map/all_to_all | solution.py:27
  17.8 157.6 %all-reduce.4.cloned.1.call-start = ((), (), s32[]{:S(2)}) async-start(), calls=%async_computation.1 | async-start | bytes 1048576 | tf_op jit(solution)/shard_map/psum | solution.py:39
  73.7 4.3 %slice-start = ((s8[8388608]{0:T(1024)(128)(4,1)}), s8[4194304]{0:T(1024)(128)(4,1)S(1)}, s32[]{:S(2)}) async-start(s8[8388608]{0:T(1024)(128)(4,1)} %bitcast.38), calls=%async_computation.2 | async-start | bytes 8388608
  76.3 3.2 slice-start.1
  79.5 11.7 %copy-start.2 = (s32[512]{0:T(512)S(1)}, s32[512]{0:T(512)}, u32[]{:S(2)}) copy-start(s32[512]{0:T(512)} %param.9) | copy-start | bytes 6148
  79.5 11.7 %copy-start.3 = (u32[128]{0:T(128)S(1)}, u32[128]{0:T(128)}, u32[]{:S(2)}) copy-start(u32[128]{0:T(128)} %constant.15) | copy-start | bytes 1540
  79.5 96.0 %copy-start = (bf16[2,512,128]{2,1,0:T(8,128)(2,1)S(1)}, bf16[2,512,128]{2,1,0:T(8,128)(2,1)}, u32[]{:S(2)}) copy-start(bf16[2,512,128]{2,1,0:T(8,128)(2,1)} %param.8) | copy-start | bytes 786436
  175.5 11.9 %slice-start.2 = ((s8[8388608]{0:T(1024)(128)(4,1)}), s8[4194304]{0:T(1024)(128)(4,1)S(1)}, s32[]{:S(2)}) async-start(s8[8388608]{0:T(1024)(128)(4,1)} %bitcast.40), calls=%async_computation.4 | async-start | bytes 8388608
  175.5 11.9 %slice-start.4 = ((s8[8388608]{0:T(1024)(128)(4,1)}), s8[4194304]{0:T(1024)(128)(4,1)S(1)}, s32[]{:S(2)}) async-start(s8[8388608]{0:T(1024)(128)(4,1)} %bitcast.42), calls=%async_computation.6 | async-start | bytes 8388608
  176.9 10.5 %slice-start.3 = ((s8[8388608]{0:T(1024)(128)(4,1)}), s8[4194304]{0:T(1024)(128)(4,1)S(1)}, s32[]{:S(2)}) async-start(s8[8388608]{0:T(1024)(128)(4,1)} %bitcast.40), calls=%async_computation.5 | async-start | bytes 8388608
  176.9 10.5 %slice-start.5 = ((s8[8388608]{0:T(1024)(128)(4,1)}), s8[4194304]{0:T(1024)(128)(4,1)S(1)}, s32[]{:S(2)}) async-start(s8[8388608]{0:T(1024)(128)(4,1)} %bitcast.42), calls=%async_computation.7 | async-start | bytes 8388608
Sparse Core Ops, SparseCore 0:
  91.2 84.1 all-reduce.3
